TPU v7x, 512 devices: a whole 4x8x8 slice. The times are simulated.
512 devices in a mesh: node: 64 (over y, z), col: 8 (over x, core).
Axes of the slice: x: 4, y: 8, z: 8, core: 2. Of those that a mesh axis runs over, the one named last changes fastest.
Arguments:
- x_t: bfloat16 [512, 32768], P('col', 'node'), may hold values from -6 to 6
- adj_tiles: bfloat16 [4096, 128, 128], P('node'), may hold values from -0.1875 to 0.1875
- tile_rows: int32 [4096], P('node'), may hold values from 0 to 3
- tile_cols: int32 [4096], P('node'), may hold values from 0 to 255, as said below
- tile_counts: int32 [64], P('node'), may hold values from 8 to 64, as said below
- w_first: bfloat16 [512, 512], P('col'), may hold values from -0.25 to 0.25
- b_first: float32 [512], P('col'), may hold values from -3 to 3
- w_second: bfloat16 [512, 512], P('col'), may hold values from -0.25 to 0.25
- b_second: float32 [512], P('col'), may hold values from -3 to 3
Outputs:
- out_t: float32 [512, 32768], P('col', 'node')
Inputs may be any that keep to these rules, and one draw needn't show every extreme that they name: `tile_cols`: column blocks q * 4 to q * 4 + 3 belong to device q of node. Among the live tiles of one device, at most 2 distinct column blocks belong to any one device, and every device's first 2 tiles name 2 distinct blocks of one device. `tile_counts`: some device has all 64 slots live.
All inputs are finite; a program needn't handle non-finite values.
Results may differ from a plain program's by a relative error of at most 0.004.
Values may be sent and summed in bfloat16 or wider, within the bound.
A program may use at most 64 MiB of HBM per device.

v0:
```python
import jax
import jax.numpy as jnp
from jax import lax
from jax.sharding import PartitionSpec as P

BLK = 128
CAP = 2


def tile_sum(x_blocks, tile_values, selector):
    products = jnp.einsum("fnj,nij->fni", x_blocks, tile_values, preferred_element_type=jnp.float32)
    return jnp.einsum("fni,nb->fbi", products, selector, precision=lax.Precision.HIGHEST)


def aggregate(feat_t, adj_tiles, tile_rows, live_count, plan):
    feat_local = feat_t.shape[0]
    row_blocks = feat_t.shape[1] // BLK
    tile_total = adj_tiles.shape[0]
    asked_of, tile_slot = plan
    own_blocks = feat_t.reshape(feat_local, row_blocks, BLK)
    outgoing = jnp.take(own_blocks, asked_of.reshape(-1), axis=1)
    incoming = lax.all_to_all(outgoing, "node", split_axis=1, concat_axis=1, tiled=True)
    x_blocks = jnp.take(incoming, tile_slot, axis=1)
    is_live = jnp.arange(tile_total, dtype=jnp.int32) < live_count
    selector = (
        (tile_rows[:, None] == jnp.arange(row_blocks, dtype=jnp.int32)[None, :]) & is_live[:, None]
    ).astype(jnp.float32)
    summed = tile_sum(x_blocks, adj_tiles, selector)
    return summed.reshape(feat_local, row_blocks * BLK).astype(jnp.bfloat16)


def dense_layer(aggregated, weight_local, bias_local):
    summed = jnp.dot(
        weight_local,
        lax.all_gather(aggregated, "col", axis=0, tiled=True),
        preferred_element_type=jnp.float32,
    )
    return summed + bias_local[:, None]


def body(x_t, adj_tiles, tile_rows, tile_cols, tile_counts, w_first, b_first, w_second, b_second):
    row_blocks = x_t.shape[1] // BLK
    peer_count = lax.axis_size("node")
    block_total = peer_count * row_blocks
    live_count = tile_counts[0]
    is_live = jnp.arange(tile_cols.shape[0], dtype=jnp.int32) < live_count
    named = (tile_cols[:, None] == jnp.arange(block_total, dtype=jnp.int32)[None, :]) & is_live[
        :, None
    ]
    needed = jnp.any(named, axis=0).astype(jnp.int32).reshape(peer_count, row_blocks)
    position = jnp.cumsum(needed, axis=1) - 1
    slot_hit = (needed[:, :, None] == 1) & (
        position[:, :, None] == jnp.arange(CAP, dtype=jnp.int32)[None, None, :]
    )
    wanted = jnp.sum(
        slot_hit.astype(jnp.int32) * jnp.arange(row_blocks, dtype=jnp.int32)[None, :, None], axis=1
    )
    asked_of = lax.all_to_all(wanted, "node", split_axis=0, concat_axis=0, tiled=True)
    owner_base = (jnp.arange(peer_count, dtype=jnp.int32) * CAP)[:, None]
    slot_table = (owner_base + jnp.clip(position, 0, CAP - 1)).reshape(-1)
    tile_slot = jnp.take(slot_table, tile_cols)
    plan = (asked_of, tile_slot)
    y_first = aggregate(x_t, adj_tiles, tile_rows, live_count, plan)
    h_first = jnp.maximum(dense_layer(y_first, w_first, b_first), 0.0).astype(jnp.bfloat16)
    y_second = aggregate(h_first, adj_tiles, tile_rows, live_count, plan)
    return dense_layer(y_second, w_second, b_second)


def solution(mesh):
    return jax.shard_map(
        body,
        mesh=mesh,
        in_specs=(
            P("col", "node"),
            P("node", None, None),
            P("node"),
            P("node"),
            P("node"),
            P("col", None),
            P("col"),
            P("col", None),
            P("col"),
        ),
        out_specs=P("col", "node"),
        check_vma=False,
    )
```

profile of v0, /device:TPU:25, one launch (start us, length us, event | category | flops | bytes accessed | tf_op | source)
XLA Modules:
  0.0 206.9 jit_solution(1067784979185888805)
XLA Ops:
  0.8 0.8 fusion.23
  1.6 0.1 reshape.72
  1.7 0.1 copy.23
  1.8 0.2 reduce_window_sum.11
  2.0 0.1 clamp_add_fusion
  2.1 0.1 copy.24
  2.2 0.7 copy.25
  2.9 15.8 %all-to-all-start = ((s32[64,1,2]{2,1,0:T(1,128)}), s32[64,1,2]{2,1,0:T(1,128)S(1)}, u32[]{:S(2)}, u32[]{:S(2)}) async-start(s32[64,1,2]{2,1,0:T(1,128)} %copy.25), calls=%async_computation | async-start | bytes 65536 | tf_op jit(solution)/shard_map/all_to_all | solution.py:58
  18.7 0.9 copy_bitcast_fusion.3
  19.6 7.5 %all-to-all-done = s32[64,1,2]{2,1,0:T(1,128)S(1)} async-done(((s32[64,1,2]{2,1,0:T(1,128)}), s32[64,1,2]{2,1,0:T(1,128)S(1)}, u32[]{:S(2)}, u32[]{:S(2)}) %all-to-all-start) | async-done | bytes 544 | tf_op jit(solution)/shard_map/all_to_all | solution.py:58
  27.1 0.5 broadcast.114
  27.6 0.7 reduce.3
  28.3 0.1 reshape.70
  28.5 2.1 %gather_fusion.1 = bf16[128,64,128]{2,1,0:T(8,128)(2,1)} fusion(bf16[64,4,128]{2,0,1:T(8,128)(2,1)S(1)} %copy_bitcast_fusion.3, s32[1024]{0:T(1024)S(1)} %pad_clamp_fusion.1), kind=kCustom, calls=%fused_computation.clone | custom fusion | bytes 4194816 | tf_op jit(solution)/shard_map/jit(_take)/gather | solution.py:21
  30.6 3.2 %select_bitcast_fusion.1 = bf16[64,128,128]{2,0,1:T(8,128)(2,1)} fusion(bf16[128,64,128]{2,1,0:T(8,128)(2,1)} %gather_fusion.1, pred[128]{0:T(512)(128)(4,1)S(1)} %compare_and_fusion.1), kind=kLoop, calls=%fused_computation.10 | loop fusion | flops 1048576 | bytes 4194432 | tf_op jit(solution)/shard_map/jit(_take)/select_n | solution.py:21
  33.8 8.0 %all-to-all-start.1 = ((bf16[64,128,128]{2,0,1:T(8,128)(2,1)}), bf16[64,128,128]{2,0,1:T(8,128)(2,1)}, u32[]{:S(2)}, u32[]{:S(2)}) async-start(bf16[64,128,128]{2,0,1:T(8,128)(2,1)} %select_bitcast_fusion.1), calls=%async_computation.1 | async-start | bytes 4194304 | tf_op jit(solution)/shard_map/all_to_all | solution.py:22
  41.8 0.1 add.63
  42.0 0.8 gather_fusion
  42.8 53.7 %all-to-all-done.1 = bf16[64,128,128]{2,0,1:T(8,128)(2,1)} async-done(((bf16[64,128,128]{2,0,1:T(8,128)(2,1)}), bf16[64,128,128]{2,0,1:T(8,128)(2,1)}, u32[]{:S(2)}, u32[]{:S(2)}) %all-to-all-start.1) | async-done | bytes 2097184 | tf_op jit(solution)/shard_map/all_to_all | solution.py:22
  96.5 2.3 %gather_fusion.2 = bf16[64,64,128]{2,1,0:T(8,128)(2,1)S(1)} fusion(bf16[64,128,128]{2,0,1:T(8,128)(2,1)} %all-to-all-done.1, s32[1024]{0:T(1024)S(1)} %pad_clamp_fusion), kind=kCustom, calls=%fused_computation.1.clone | custom fusion | bytes 2097408 | tf_op jit(solution)/shard_map/jit(_take)/gather | solution.py:23
  98.8 1.5 convolution_bitcast_fusion.1
  100.4 2.0 fusion.7
  102.4 15.1 %all_gather.6 = bf16[512,512]{1,0:T(8,128)(2,1)S(1)} all-gather(bf16[64,512]{1,0:T(8,128)(2,1)S(1)} %bitcast.53), channel_id=1, replica_groups=mesh['node'=64,'col'=8] {'col'}, dimensions={0}, use_global_device_ids=true | all-gather | bytes 589824 | tf_op jit(solution)/shard_map/all_gather | solution.py:35
  117.5 0.2 fusion.13
  117.7 2.2 %gather_fusion.3 = bf16[128,64,128]{2,1,0:T(8,128)(2,1)} fusion(bf16[64,4,128]{2,0,1:T(8,128)(2,1)S(1)} %bitcast.50, s32[1024]{0:T(1024)S(1)} %pad_clamp_fusion.1), kind=kCustom, calls=%fused_computation.2.clone | custom fusion | bytes 4194816 | tf_op jit(solution)/shard_map/jit(_take)/gather | solution.py:21
  119.9 1.9 select_bitcast_fusion
  121.7 62.4 %all_to_all.19 = bf16[64,128,128]{2,0,1:T(8,128)(2,1)} all-to-all(bf16[64,128,128]{2,0,1:T(8,128)(2,1)S(1)} %select_bitcast_fusion), channel_id=1, replica_groups=mesh['node'=64,'col'=8] {'node'}, dimensions={1} | all-to-all | bytes 4194304 | tf_op jit(solution)/shard_map/all_to_all | solution.py:22
  184.1 2.3 %gather_fusion.4 = bf16[64,64,128]{2,1,0:T(8,128)(2,1)S(1)} fusion(bf16[64,128,128]{2,0,1:T(8,128)(2,1)} %all_to_all.19, s32[1024]{0:T(1024)S(1)} %pad_clamp_fusion), kind=kCustom, calls=%fused_computation.3.clone | custom fusion | bytes 2097408 | tf_op jit(solution)/shard_map/jit(_take)/gather | solution.py:23
  186.4 1.5 convolution_bitcast_fusion
  188.0 2.0 fusion.10
  190.0 16.0 %all_gather.7 = bf16[512,512]{1,0:T(8,128)(2,1)S(1)} all-gather(bf16[64,512]{1,0:T(8,128)(2,1)S(1)} %bitcast.54), channel_id=1, replica_groups=mesh['node'=64,'col'=8] {'col'}, dimensions={0}, use_global_device_ids=true | all-gather | bytes 589824 | tf_op jit(solution)/shard_map/all_gather | solution.py:35
  206.0 0.9 fusion.4
  (29 shorter events, 0.2 us)
Async XLA Ops:
  0.0 98.8 %copy-start = (bf16[64,128,128]{2,1,0:T(8,128)(2,1)S(1)}, bf16[64,128,128]{2,1,0:T(8,128)(2,1)}, u32[]{:S(2)}) copy-start(bf16[64,128,128]{2,1,0:T(8,128)(2,1)} %param.14) | copy-start | bytes 6291460
  2.9 24.2 %all-to-all-start = ((s32[64,1,2]{2,1,0:T(1,128)}), s32[64,1,2]{2,1,0:T(1,128)S(1)}, u32[]{:S(2)}, u32[]{:S(2)}) async-start(s32[64,1,2]{2,1,0:T(1,128)} %copy.25), calls=%async_computation | async-start | bytes 65536 | tf_op jit(solution)/shard_map/all_to_all | solution.py:58
  33.8 8.1 %copy-start.5 = (s32[64]{0:T(128)S(1)}, s32[64]{0:T(128)}, u32[]{:S(2)}) copy-start(s32[64]{0:T(128)} %param.16) | copy-start | bytes 772
  33.8 62.7 %all-to-all-start.1 = ((bf16[64,128,128]{2,0,1:T(8,128)(2,1)}), bf16[64,128,128]{2,0,1:T(8,128)(2,1)}, u32[]{:S(2)}, u32[]{:S(2)}) async-start(bf16[64,128,128]{2,0,1:T(8,128)(2,1)} %select_bitcast_fusion.1), calls=%async_computation.1 | async-start | bytes 4194304 | tf_op jit(solution)/shard_map/all_to_all | solution.py:22
  98.8 1.6 copy-start.3
  100.4 17.1 %copy-start.1 = (bf16[64,512]{1,0:T(8,128)(2,1)S(1)}, bf16[64,512]{1,0:T(8,128)(2,1)}, u32[]{:S(2)}) copy-start(bf16[64,512]{1,0:T(8,128)(2,1)} %param.18) | copy-start | bytes 196612
  100.4 17.1 %copy-start.6 = (f32[64]{0:T(128)S(1)}, f32[64]{0:T(128)}, u32[]{:S(2)}) copy-start(f32[64]{0:T(128)} %param.19) | copy-start | bytes 772
  188.0 18.1 %copy-start.2 = (bf16[64,512]{1,0:T(8,128)(2,1)S(1)}, bf16[64,512]{1,0:T(8,128)(2,1)}, u32[]{:S(2)}) copy-start(bf16[64,512]{1,0:T(8,128)(2,1)} %param.20) | copy-start | bytes 196612
  188.0 18.0 %copy-start.4 = (f32[64]{0:T(128)S(1)}, f32[64]{0:T(128)}, u32[]{:S(2)}) copy-start(f32[64]{0:T(128)} %param.21) | copy-start | bytes 772
where the time goes:
time: 207 us
  blocking collectives  93.5 us (45%)
  waiting for transfers between devices  61.2 us (30%)
  starting transfers between devices  23.9 us (12%)
  local copies, waits for them, and re-layouts  12.4 us (6%)
  matrix products  8.07 us (4%)
  other arithmetic  6.84 us (3%)
    all_to_all x1, blocking collectives, aggregate(): lax.all_to_all(outgoing, 'node', split_axis=1, concat_axis=1, tiled=True)  62.4 us
    all_to_all x1, waiting for transfers between devices, aggregate(): lax.all_to_all(outgoing, 'node', split_axis=1, concat_axis=1, tiled=True)  53.7 us
    all_gather x2, blocking collectives, dense_layer(): lax.all_gather(aggregated, 'col', axis=0, tiled=True)  31.1 us
    all_to_all x1, starting transfers between devices, body(): lax.all_to_all(wanted, 'node', split_axis=0, concat_axis=0, tiled=True)  15.8 us
    all_to_all x1, starting transfers between devices, aggregate(): lax.all_to_all(outgoing, 'node', split_axis=1, concat_axis=1, tiled=True)  8.02 us
    all_to_all x1, waiting for transfers between devices, body(): lax.all_to_all(wanted, 'node', split_axis=0, concat_axis=0, tiled=True)  7.51 us
    select_n x3, other arithmetic, aggregate(): outgoing = jnp.take(own_blocks, asked_of.reshape(-1), axis=1)  5.01 us
    gather x2, local copies, waits for them, and re-layouts, aggregate(): x_blocks = jnp.take(incoming, tile_slot, axis=1)  4.68 us
  transfers between devices with their start and end apart: 2, of which 2 were waited for; matrix products, arithmetic and copies ran while one was open for 1% of the time, Pallas kernels for 0%

commit v1 on v0

--- a/solution.py
+++ b/solution.py
@@ -1,10 +1,43 @@
+import functools
 import jax
 import jax.numpy as jnp
 from jax import lax
 from jax.sharding import PartitionSpec as P
+from jax.lax import axis_index, axis_size, ppermute
 
 BLK = 128
 CAP = 2
+
+
+def answer_strings(vec, row_axis):
+    current_value = axis_size(row_axis)
+    kept_arr = axis_index(row_axis)
+    block_next, finding, piece_now = (current_value, kept_arr, vec.shape[0])
+    cards = [i0 * block_next if j0 == 0 else i0 for j0, i0 in enumerate(vec.shape)]
+    v_now = lax.dynamic_update_slice_in_dim(
+        jnp.zeros(cards, vec.dtype), vec, finding * piece_now, axis=0
+    )
+    z2 = later = vec
+    for to_i in range(1, block_next // 2 + 1):
+        val = range(block_next)
+        reply = map(lambda j0: (j0, (j0 + 1) % block_next), val)
+        h_now = list(reply)
+        z2 = ppermute(z2, axis_name=row_axis, perm=h_now)
+        v_now = lax.dynamic_update_slice_in_dim(
+            v_now, z2, (finding - to_i) % block_next * piece_now, axis=0
+        )
+        if 2 * to_i < block_next:
+            all_values = range(block_next)
+            found_now = map(lambda j0: (j0, (j0 - 1) % block_next), all_values)
+            odd = list(found_now)
+            later = ppermute(later, axis_name=row_axis, perm=odd)
+            v_now = lax.dynamic_update_slice_in_dim(
+                v_now, later, (finding + to_i) % block_next * piece_now, axis=0
+            )
+    return v_now
+
+
+group_assign = functools.partial(answer_strings, row_axis="col")
 
 
 def tile_sum(x_blocks, tile_values, selector):
@@ -30,11 +63,7 @@
 
 
 def dense_layer(aggregated, weight_local, bias_local):
-    summed = jnp.dot(
-        weight_local,
-        lax.all_gather(aggregated, "col", axis=0, tiled=True),
-        preferred_element_type=jnp.float32,
-    )
+    summed = jnp.dot(weight_local, group_assign(aggregated), preferred_element_type=jnp.float32)
     return summed + bias_local[:, None]
 
 

time: 207 us -> 215 us (1.039); the launches traced: 207 us -> 211 us
  blocking collectives: 93.5 us -> 59.9 us
  starting transfers between devices: 23.9 us -> 47.8 us
  waiting for transfers between devices: 61.2 us -> 74.7 us
    all_gather x2 -> x0, blocking collectives: 31.1 us -> none  [dense_layer(): lax.all_gather(aggregated, 'col', axis=0, tiled=True)]
    ppermute x0 -> x14, starting transfers between devices: none -> 24 us  [the longest x8 15.8 us: answer_strings(): z2 = ppermute(z2, axis_name=row_axis, perm=h_now)]
    ppermute x0 -> x14, waiting for transfers between devices: none -> 13.7 us  [the longest x8 12.9 us: answer_strings(): z2 = ppermute(z2, axis_name=row_axis, perm=h_now)]
    all_to_all x1, blocking collectives: 62.4 us -> 59.9 us  [aggregate(): lax.all_to_all(outgoing, 'node', split_axis=1, concat_axis=1, tiled=True)]
  transfers between devices with their start and end apart: 2 -> 16, of which waited for: 2 -> 13; matrix products, arithmetic and copies ran while one was open for 1% -> 1% of each run, Pallas kernels for 0% -> 0%
where the time goes in v1:
time: 215 us; the launch traced here: 211 us
  waiting for transfers between devices  74.7 us (35%)
  blocking collectives  59.9 us (28%)
  starting transfers between devices  47.8 us (22%)
  local copies, waits for them, and re-layouts  12.6 us (6%)
  matrix products  8.07 us (4%)
  other arithmetic  6.85 us (3%)
    all_to_all x1, blocking collectives, aggregate(): lax.all_to_all(outgoing, 'node', split_axis=1, concat_axis=1, tiled=True)  59.9 us
    all_to_all x1, waiting for transfers between devices, aggregate(): lax.all_to_all(outgoing, 'node', split_axis=1, concat_axis=1, tiled=True)  53.5 us
    all_to_all x1, starting transfers between devices, body(): lax.all_to_all(wanted, 'node', split_axis=0, concat_axis=0, tiled=True)  15.8 us
    ppermute x8, starting transfers between devices, answer_strings(): z2 = ppermute(z2, axis_name=row_axis, perm=h_now)  15.8 us
    ppermute x8, waiting for transfers between devices, answer_strings(): z2 = ppermute(z2, axis_name=row_axis, perm=h_now)  12.9 us
    ppermute x6, starting transfers between devices, answer_strings(): later = ppermute(later, axis_name=row_axis, perm=odd)  8.18 us
    all_to_all x1, starting transfers between devices, aggregate(): lax.all_to_all(outgoing, 'node', split_axis=1, concat_axis=1, tiled=True)  8.01 us
    all_to_all x1, waiting for transfers between devices, body(): lax.all_to_all(wanted, 'node', split_axis=0, concat_axis=0, tiled=True)  7.51 us
  transfers between devices with their start and end apart: 16, of which 13 were waited for; matrix products, arithmetic and copies ran while one was open for 1% of the time, Pallas kernels for 0%

profile of v1, /device:TPU:25, one launch (start us, length us, event | category | flops | bytes accessed | tf_op | source)
XLA Modules:
  0.0 211.3 jit_solution(11272574395846269757)
XLA Ops:
  2.9 15.8 %all-to-all-start = ((s32[64,1,2]{2,1,0:T(1,128)}), s32[64,1,2]{2,1,0:T(1,128)S(1)}, u32[]{:S(2)}, u32[]{:S(2)}) async-start(s32[64,1,2]{2,1,0:T(1,128)} %copy.25), calls=%async_computation | async-start | bytes 65536 | tf_op jit(solution)/shard_map/all_to_all | solution.py:87
  18.7 0.9 copy_bitcast_fusion.3
  19.6 7.5 %all-to-all-done = s32[64,1,2]{2,1,0:T(1,128)S(1)} async-done(((s32[64,1,2]{2,1,0:T(1,128)}), s32[64,1,2]{2,1,0:T(1,128)S(1)}, u32[]{:S(2)}, u32[]{:S(2)}) %all-to-all-start) | async-done | bytes 544 | tf_op jit(solution)/shard_map/all_to_all | solution.py:87
  28.5 2.1 %gather_fusion.1 = bf16[128,64,128]{2,1,0:T(8,128)(2,1)} fusion(bf16[64,4,128]{2,0,1:T(8,128)(2,1)S(1)} %copy_bitcast_fusion.3, s32[1024]{0:T(1024)S(1)} %pad_clamp_fusion.1), kind=kCustom, calls=%fused_computation.clone | custom fusion | bytes 4194816 | tf_op jit(solution)/shard_map/jit(_take)/gather | solution.py:54
  30.7 3.2 %select_bitcast_fusion.1 = bf16[64,128,128]{2,0,1:T(8,128)(2,1)} fusion(bf16[128,64,128]{2,1,0:T(8,128)(2,1)} %gather_fusion.1, pred[128]{0:T(512)(128)(4,1)S(1)} %compare_and_fusion.1), kind=kLoop, calls=%fused_computation.10 | loop fusion | flops 1048576 | bytes 4194432 | tf_op jit(solution)/shard_map/jit(_take)/select_n | solution.py:54
  33.8 8.0 %all-to-all-start.1 = ((bf16[64,128,128]{2,0,1:T(8,128)(2,1)}), bf16[64,128,128]{2,0,1:T(8,128)(2,1)}, u32[]{:S(2)}, u32[]{:S(2)}) async-start(bf16[64,128,128]{2,0,1:T(8,128)(2,1)} %select_bitcast_fusion.1), calls=%async_computation.1 | async-start | bytes 4194304 | tf_op jit(solution)/shard_map/all_to_all | solution.py:55
  42.1 0.8 gather_fusion
  43.0 53.5 %all-to-all-done.1 = bf16[64,128,128]{2,0,1:T(8,128)(2,1)} async-done(((bf16[64,128,128]{2,0,1:T(8,128)(2,1)}), bf16[64,128,128]{2,0,1:T(8,128)(2,1)}, u32[]{:S(2)}, u32[]{:S(2)}) %all-to-all-start.1) | async-done | bytes 2097184 | tf_op jit(solution)/shard_map/all_to_all | solution.py:55
  96.5 2.3 %gather_fusion.2 = bf16[64,64,128]{2,1,0:T(8,128)(2,1)S(1)} fusion(bf16[64,128,128]{2,0,1:T(8,128)(2,1)} %all-to-all-done.1, s32[1024]{0:T(1024)S(1)} %pad_clamp_fusion), kind=kCustom, calls=%fused_computation.1.clone | custom fusion | bytes 2097408 | tf_op jit(solution)/shard_map/jit(_take)/gather | solution.py:56
  98.9 1.5 convolution_bitcast_fusion.1
  100.4 2.0 fusion.7
  102.4 2.9 %collective-permute-start = (bf16[64,512]{1,0:T(8,128)(2,1)S(1)}, bf16[64,512]{1,0:T(8,128)(2,1)S(1)}, u32[]{:S(2)}, u32[]{:S(2)}) collective-permute-start(bf16[64,512]{1,0:T(8,128)(2,1)S(1)} %bitcast.61), channel_id=1, source_target_pairs={{0,1},{1,2},{2,3},{3,4},{4,5},{5,6},{6,7},{7,0},{8,9},{9,10},{10,1... | collective-permute-start | bytes 196616 | tf_op jit(solution)/shard_map/ppermute | solution.py:25
  105.4 1.3 collective-permute-done
  106.6 2.4 %collective-permute-start.2 = (bf16[64,512]{1,0:T(8,128)(2,1)S(1)}, bf16[64,512]{1,0:T(8,128)(2,1)S(1)}, u32[]{:S(2)}, u32[]{:S(2)}) collective-permute-start(bf16[64,512]{1,0:T(8,128)(2,1)S(1)} %collective-permute-done), channel_id=1, source_target_pairs={{0,1},{1,2},{2,3},{3,4},{4,5},{5,6},{6,7},{7,0},{8,9},{9,10},{10,1... | collective-permute-start | bytes 196616 | tf_op jit(solution)/shard_map/ppermute | solution.py:25
  109.2 1.2 collective-permute-done.2
  110.3 2.4 %collective-permute-start.4 = (bf16[64,512]{1,0:T(8,128)(2,1)S(1)}, bf16[64,512]{1,0:T(8,128)(2,1)S(1)}, u32[]{:S(2)}, u32[]{:S(2)}) collective-permute-start(bf16[64,512]{1,0:T(8,128)(2,1)S(1)} %collective-permute-done.2), channel_id=1, source_target_pairs={{0,1},{1,2},{2,3},{3,4},{4,5},{5,6},{6,7},{7,0},{8,9},{9,10},{10,1... | collective-permute-start | bytes 196616 | tf_op jit(solution)/shard_map/ppermute | solution.py:25
  113.0 1.0 collective-permute-start.5
  114.8 1.6 collective-permute-start.6
  116.7 3.0 %collective-permute-done.6 = bf16[64,512]{1,0:T(8,128)(2,1)S(1)} collective-permute-done((bf16[64,512]{1,0:T(8,128)(2,1)S(1)}, bf16[64,512]{1,0:T(8,128)(2,1)S(1)}, u32[]{:S(2)}, u32[]{:S(2)}) %collective-permute-start.6) | collective-permute-done | bytes 65568 | tf_op jit(solution)/shard_map/ppermute | solution.py:25
  119.9 2.1 %gather_fusion.3 = bf16[128,64,128]{2,1,0:T(8,128)(2,1)} fusion(bf16[64,4,128]{2,0,1:T(8,128)(2,1)S(1)} %bitcast.54, s32[1024]{0:T(1024)S(1)} %pad_clamp_fusion.1), kind=kCustom, calls=%fused_computation.2.clone | custom fusion | bytes 4194816 | tf_op jit(solution)/shard_map/jit(_take)/gather | solution.py:54
  122.1 1.9 select_bitcast_fusion
  123.9 59.9 %all_to_all.19 = bf16[64,128,128]{2,0,1:T(8,128)(2,1)} all-to-all(bf16[64,128,128]{2,0,1:T(8,128)(2,1)S(1)} %select_bitcast_fusion), channel_id=1, replica_groups=mesh['node'=64,'col'=8] {'node'}, dimensions={1} | all-to-all | bytes 4194304 | tf_op jit(solution)/shard_map/all_to_all | solution.py:55
  183.8 2.3 %gather_fusion.4 = bf16[64,64,128]{2,1,0:T(8,128)(2,1)S(1)} fusion(bf16[64,128,128]{2,0,1:T(8,128)(2,1)} %all_to_all.19, s32[1024]{0:T(1024)S(1)} %pad_clamp_fusion), kind=kCustom, calls=%fused_computation.3.clone | custom fusion | bytes 2097408 | tf_op jit(solution)/shard_map/jit(_take)/gather | solution.py:56
  186.2 1.5 convolution_bitcast_fusion
  187.8 2.0 fusion.10
  189.7 4.1 %collective-permute-start.7 = (bf16[64,512]{1,0:T(8,128)(2,1)S(1)}, bf16[64,512]{1,0:T(8,128)(2,1)S(1)}, u32[]{:S(2)}, u32[]{:S(2)}) collective-permute-start(bf16[64,512]{1,0:T(8,128)(2,1)S(1)} %bitcast.59), channel_id=1, source_target_pairs={{0,1},{1,2},{2,3},{3,4},{4,5},{5,6},{6,7},{7,0},{8,9},{9,10},{10,1... | collective-permute-start | bytes 196616 | tf_op jit(solution)/shard_map/ppermute | solution.py:25
  193.8 1.1 collective-permute-start.8
  195.7 1.8 collective-permute-start.9
  197.6 2.3 %collective-permute-start.10 = (bf16[64,512]{1,0:T(8,128)(2,1)S(1)}, bf16[64,512]{1,0:T(8,128)(2,1)S(1)}, u32[]{:S(2)}, u32[]{:S(2)}) collective-permute-start(bf16[64,512]{1,0:T(8,128)(2,1)S(1)} %collective-permute-done.8), channel_id=1, source_target_pairs={{0,7},{1,0},{2,1},{3,2},{4,3},{5,4},{6,5},{7,6},{8,15},{9,8},{10,9... | collective-permute-start | bytes 196616 | tf_op jit(solution)/shard_map/ppermute | solution.py:33
  201.3 3.5 %collective-permute-start.12 = (bf16[64,512]{1,0:T(8,128)(2,1)S(1)}, bf16[64,512]{1,0:T(8,128)(2,1)S(1)}, u32[]{:S(2)}, u32[]{:S(2)}) collective-permute-start(bf16[64,512]{1,0:T(8,128)(2,1)S(1)} %collective-permute-done.10), channel_id=1, source_target_pairs={{0,7},{1,0},{2,1},{3,2},{4,3},{5,4},{6,5},{7,6},{8,15},{9,8},{10,9... | collective-permute-start | bytes 196616 | tf_op jit(solution)/shard_map/ppermute | solution.py:33
  205.7 4.7 %collective-permute-done.13 = bf16[64,512]{1,0:T(8,128)(2,1)S(1)} collective-permute-done((bf16[64,512]{1,0:T(8,128)(2,1)S(1)}, bf16[64,512]{1,0:T(8,128)(2,1)S(1)}, u32[]{:S(2)}, u32[]{:S(2)}) %collective-permute-start.13) | collective-permute-done | bytes 65568 | tf_op jit(solution)/shard_map/ppermute | solution.py:25
  210.4 0.9 fusion.4
  (73 shorter events, 8.4 us)
Async XLA Ops:
  0.0 98.8 %copy-start = (bf16[64,128,128]{2,1,0:T(8,128)(2,1)S(1)}, bf16[64,128,128]{2,1,0:T(8,128)(2,1)}, u32[]{:S(2)}) copy-start(bf16[64,128,128]{2,1,0:T(8,128)(2,1)} %param.14) | copy-start | bytes 6291460
  2.9 24.2 %all-to-all-start = ((s32[64,1,2]{2,1,0:T(1,128)}), s32[64,1,2]{2,1,0:T(1,128)S(1)}, u32[]{:S(2)}, u32[]{:S(2)}) async-start(s32[64,1,2]{2,1,0:T(1,128)} %copy.25), calls=%async_computation | async-start | bytes 65536 | tf_op jit(solution)/shard_map/all_to_all | solution.py:87
  33.8 8.3 %copy-start.5 = (s32[64]{0:T(128)S(1)}, s32[64]{0:T(128)}, u32[]{:S(2)}) copy-start(s32[64]{0:T(128)} %param.16) | copy-start | bytes 772
  33.8 62.7 %all-to-all-start.1 = ((bf16[64,128,128]{2,0,1:T(8,128)(2,1)}), bf16[64,128,128]{2,0,1:T(8,128)(2,1)}, u32[]{:S(2)}, u32[]{:S(2)}) async-start(bf16[64,128,128]{2,0,1:T(8,128)(2,1)} %select_bitcast_fusion.1), calls=%async_computation.1 | async-start | bytes 4194304 | tf_op jit(solution)/shard_map/all_to_all | solution.py:55
  98.8 1.6 copy-start.3
  100.4 19.3 %copy-start.1 = (bf16[64,512]{1,0:T(8,128)(2,1)S(1)}, bf16[64,512]{1,0:T(8,128)(2,1)}, u32[]{:S(2)}) copy-start(bf16[64,512]{1,0:T(8,128)(2,1)} %param.18) | copy-start | bytes 196612
  100.4 19.3 %copy-start.6 = (f32[64]{0:T(128)S(1)}, f32[64]{0:T(128)}, u32[]{:S(2)}) copy-start(f32[64]{0:T(128)} %param.19) | copy-start | bytes 772
  102.4 4.2 %collective-permute-start = (bf16[64,512]{1,0:T(8,128)(2,1)S(1)}, bf16[64,512]{1,0:T(8,128)(2,1)S(1)}, u32[]{:S(2)}, u32[]{:S(2)}) collective-permute-start(bf16[64,512]{1,0:T(8,128)(2,1)S(1)} %bitcast.61), channel_id=1, source_target_pairs={{0,1},{1,2},{2,3},{3,4},{4,5},{5,6},{6,7},{7,0},{8,9},{9,10},{10,1... | collective-permute-start | bytes 196616 | tf_op jit(solution)/shard_map/ppermute | solution.py:25
  105.3 3.7 %collective-permute-start.1 = (bf16[64,512]{1,0:T(8,128)(2,1)S(1)}, bf16[64,512]{1,0:T(8,128)(2,1)S(1)}, u32[]{:S(2)}, u32[]{:S(2)}) collective-permute-start(bf16[64,512]{1,0:T(8,128)(2,1)S(1)} %bitcast.62), channel_id=1, source_target_pairs={{0,7},{1,0},{2,1},{3,2},{4,3},{5,4},{6,5},{7,6},{8,15},{9,8},{10,9... | collective-permute-start | bytes 196616 | tf_op jit(solution)/shard_map/ppermute | solution.py:33
  106.6 3.7 %collective-permute-start.2 = (bf16[64,512]{1,0:T(8,128)(2,1)S(1)}, bf16[64,512]{1,0:T(8,128)(2,1)S(1)}, u32[]{:S(2)}, u32[]{:S(2)}) collective-permute-start(bf16[64,512]{1,0:T(8,128)(2,1)S(1)} %collective-permute-done), channel_id=1, source_target_pairs={{0,1},{1,2},{2,3},{3,4},{4,5},{5,6},{6,7},{7,0},{8,9},{9,10},{10,1... | collective-permute-start | bytes 196616 | tf_op jit(solution)/shard_map/ppermute | solution.py:25
  109.0 4.0 %collective-permute-start.3 = (bf16[64,512]{1,0:T(8,128)(2,1)S(1)}, bf16[64,512]{1,0:T(8,128)(2,1)S(1)}, u32[]{:S(2)}, u32[]{:S(2)}) collective-permute-start(bf16[64,512]{1,0:T(8,128)(2,1)S(1)} %collective-permute-done.1), channel_id=1, source_target_pairs={{0,7},{1,0},{2,1},{3,2},{4,3},{5,4},{6,5},{7,6},{8,15},{9,8},{10,9... | collective-permute-start | bytes 196616 | tf_op jit(solution)/shard_map/ppermute | solution.py:33
  110.3 4.4 %collective-permute-start.4 = (bf16[64,512]{1,0:T(8,128)(2,1)S(1)}, bf16[64,512]{1,0:T(8,128)(2,1)S(1)}, u32[]{:S(2)}, u32[]{:S(2)}) collective-permute-start(bf16[64,512]{1,0:T(8,128)(2,1)S(1)} %collective-permute-done.2), channel_id=1, source_target_pairs={{0,1},{1,2},{2,3},{3,4},{4,5},{5,6},{6,7},{7,0},{8,9},{9,10},{10,1... | collective-permute-start | bytes 196616 | tf_op jit(solution)/shard_map/ppermute | solution.py:25
  113.0 3.7 %collective-permute-start.5 = (bf16[64,512]{1,0:T(8,128)(2,1)S(1)}, bf16[64,512]{1,0:T(8,128)(2,1)S(1)}, u32[]{:S(2)}, u32[]{:S(2)}) collective-permute-start(bf16[64,512]{1,0:T(8,128)(2,1)S(1)} %collective-permute-done.3), channel_id=1, source_target_pairs={{0,7},{1,0},{2,1},{3,2},{4,3},{5,4},{6,5},{7,6},{8,15},{9,8},{10,9... | collective-permute-start | bytes 196616 | tf_op jit(solution)/shard_map/ppermute | solution.py:33
  114.8 4.9 %collective-permute-start.6 = (bf16[64,512]{1,0:T(8,128)(2,1)S(1)}, bf16[64,512]{1,0:T(8,128)(2,1)S(1)}, u32[]{:S(2)}, u32[]{:S(2)}) collective-permute-start(bf16[64,512]{1,0:T(8,128)(2,1)S(1)} %collective-permute-done.4), channel_id=1, source_target_pairs={{0,1},{1,2},{2,3},{3,4},{4,5},{5,6},{6,7},{7,0},{8,9},{9,10},{10,1... | collective-permute-start | bytes 196616 | tf_op jit(solution)/shard_map/ppermute | solution.py:25
  187.7 22.7 %copy-start.2 = (bf16[64,512]{1,0:T(8,128)(2,1)S(1)}, bf16[64,512]{1,0:T(8,128)(2,1)}, u32[]{:S(2)}) copy-start(bf16[64,512]{1,0:T(8,128)(2,1)} %param.20) | copy-start | bytes 196612
  187.7 22.7 %copy-start.4 = (f32[64]{0:T(128)S(1)}, f32[64]{0:T(128)}, u32[]{:S(2)}) copy-start(f32[64]{0:T(128)} %param.21) | copy-start | bytes 772
  189.7 6.0 %collective-permute-start.7 = (bf16[64,512]{1,0:T(8,128)(2,1)S(1)}, bf16[64,512]{1,0:T(8,128)(2,1)S(1)}, u32[]{:S(2)}, u32[]{:S(2)}) collective-permute-start(bf16[64,512]{1,0:T(8,128)(2,1)S(1)} %bitcast.59), channel_id=1, source_target_pairs={{0,1},{1,2},{2,3},{3,4},{4,5},{5,6},{6,7},{7,0},{8,9},{9,10},{10,1... | collective-permute-start | bytes 196616 | tf_op jit(solution)/shard_map/ppermute | solution.py:25
  193.8 3.7 %collective-permute-start.8 = (bf16[64,512]{1,0:T(8,128)(2,1)S(1)}, bf16[64,512]{1,0:T(8,128)(2,1)S(1)}, u32[]{:S(2)}, u32[]{:S(2)}) collective-permute-start(bf16[64,512]{1,0:T(8,128)(2,1)S(1)} %bitcast.60), channel_id=1, source_target_pairs={{0,7},{1,0},{2,1},{3,2},{4,3},{5,4},{6,5},{7,6},{8,15},{9,8},{10,9... | collective-permute-start | bytes 196616 | tf_op jit(solution)/shard_map/ppermute | solution.py:33
  195.7 4.9 %collective-permute-start.9 = (bf16[64,512]{1,0:T(8,128)(2,1)S(1)}, bf16[64,512]{1,0:T(8,128)(2,1)S(1)}, u32[]{:S(2)}, u32[]{:S(2)}) collective-permute-start(bf16[64,512]{1,0:T(8,128)(2,1)S(1)} %collective-permute-done.7), channel_id=1, source_target_pairs={{0,1},{1,2},{2,3},{3,4},{4,5},{5,6},{6,7},{7,0},{8,9},{9,10},{10,1... | collective-permute-start | bytes 196616 | tf_op jit(solution)/shard_map/ppermute | solution.py:25
  197.6 3.7 %collective-permute-start.10 = (bf16[64,512]{1,0:T(8,128)(2,1)S(1)}, bf16[64,512]{1,0:T(8,128)(2,1)S(1)}, u32[]{:S(2)}, u32[]{:S(2)}) collective-permute-start(bf16[64,512]{1,0:T(8,128)(2,1)S(1)} %collective-permute-done.8), channel_id=1, source_target_pairs={{0,7},{1,0},{2,1},{3,2},{4,3},{5,4},{6,5},{7,6},{8,15},{9,8},{10,9... | collective-permute-start | bytes 196616 | tf_op jit(solution)/shard_map/ppermute | solution.py:33
  200.6 4.9 %collective-permute-start.11 = (bf16[64,512]{1,0:T(8,128)(2,1)S(1)}, bf16[64,512]{1,0:T(8,128)(2,1)S(1)}, u32[]{:S(2)}, u32[]{:S(2)}) collective-permute-start(bf16[64,512]{1,0:T(8,128)(2,1)S(1)} %collective-permute-done.9), channel_id=1, source_target_pairs={{0,1},{1,2},{2,3},{3,4},{4,5},{5,6},{6,7},{7,0},{8,9},{9,10},{10,1... | collective-permute-start | bytes 196616 | tf_op jit(solution)/shard_map/ppermute | solution.py:25
  201.3 4.4 %collective-permute-start.12 = (bf16[64,512]{1,0:T(8,128)(2,1)S(1)}, bf16[64,512]{1,0:T(8,128)(2,1)S(1)}, u32[]{:S(2)}, u32[]{:S(2)}) collective-permute-start(bf16[64,512]{1,0:T(8,128)(2,1)S(1)} %collective-permute-done.10), channel_id=1, source_target_pairs={{0,7},{1,0},{2,1},{3,2},{4,3},{5,4},{6,5},{7,6},{8,15},{9,8},{10,9... | collective-permute-start | bytes 196616 | tf_op jit(solution)/shard_map/ppermute | solution.py:33
  205.5 4.9 %collective-permute-start.13 = (bf16[64,512]{1,0:T(8,128)(2,1)S(1)}, bf16[64,512]{1,0:T(8,128)(2,1)S(1)}, u32[]{:S(2)}, u32[]{:S(2)}) collective-permute-start(bf16[64,512]{1,0:T(8,128)(2,1)S(1)} %collective-permute-done.11), channel_id=1, source_target_pairs={{0,1},{1,2},{2,3},{3,4},{4,5},{5,6},{6,7},{7,0},{8,9},{9,10},{10,1... | collective-permute-start | bytes 196616 | tf_op jit(solution)/shard_map/ppermute | solution.py:25
